TPU v7x, 256 devices: a whole 4x4x8 slice. The times are simulated.
256 devices in a mesh: row: 32 (over z, y_lo, core), col: 8 (over y_hi, x).
Axes of the slice: x: 4, y: 4 (y_hi: 2, y_lo: 2; y = y_hi * 2 + y_lo), z: 8, core: 2. Of those that a mesh axis runs over, the one named last changes fastest.
Arguments:
- features: bfloat16 [32768, 128], P(('col', 'row')), may hold values from -96 to 96
- weight: bfloat16 [128, 256], replicated, may hold values from -0.5 to 0.5
- bias: float32 [256], replicated, may hold values from -3 to 3
- cotangent: bfloat16 [32768, 256], P(('row', 'col')), may hold values from -6 to 6
- tile_values: bfloat16 [32, 8, 256, 128, 128], P('row', 'col'), may hold values from 0 to 4, as said below
- tile_pos: int32 [32, 8, 2, 256], P('row', 'col'), may hold values from 0 to 31, as said below
- tile_count: int32 [32, 8], P('row', 'col'), may hold values from 0 to 256, as said below
- block_perm: int32 [256], replicated, may hold values from 0 to 255, as said below
Outputs:
- hidden: bfloat16 [32768, 256], P(('row', 'col'))
- weight_grad: float32 [128, 256], replicated
- bias_grad: float32 [256], replicated
Inputs may be any that keep to these rules, and one draw needn't show every extreme that they name: `tile_values`: entries are 0 or a weight of at least 0.25; slots t at or beyond tile_count[r, c] belong to no tile. `tile_pos`: entry [r, c, 0, t] is the slot's tile row, below 8, within row block r, and [r, c, 1, t] its tile column, below 32, within column block c, both in the reordered numbering; the slots of one cell hold distinct positions. `tile_count`: every draw has a cell with 256 live slots. `block_perm`: each aligned run of 8 entries is a permutation of that run's own indices.
All inputs are finite; a program needn't handle non-finite values.
Results may differ from a plain program's by a relative error of at most 0.0059.
Values may be sent and summed in bfloat16 or wider, within the bound.
No kernel may reach another device: no remote copies, remote signals or barrier semaphores. Data moves between devices by JAX's collectives and lax.ppermute only.
A program may use at most 64 MiB of HBM per device.

v0:
```python
import jax
import jax.numpy as jnp
from jax import lax
from jax.sharding import PartitionSpec as P


def local_index(block_perm, tile_axis, block_index, run_length):
    return jnp.take(block_perm, block_index * run_length + tile_axis) - block_index * run_length


def body(features, weight, bias, cotangent, tile_values, tile_pos, tile_count, block_perm):
    row_count = lax.axis_size("row")
    col_count = lax.axis_size("col")
    row_index = lax.axis_index("row")
    col_index = lax.axis_index("col")
    packed = tile_values[0, 0]
    positions = tile_pos[0, 0]
    live_count = tile_count[0, 0]
    max_tiles = packed.shape[0]
    tile_size = packed.shape[1]
    feat_width = features.shape[1]
    row_tiles = block_perm.shape[0] // row_count
    col_tiles = row_tiles * row_count // col_count
    block_tiles = min(64, max_tiles)
    lane_index = jnp.arange(block_tiles, dtype=jnp.int32)
    own_rows = local_index(block_perm, positions[0], row_index, row_tiles)
    own_cols = local_index(block_perm, positions[1], col_index, col_tiles)

    def degree_step(block_step, totals):
        row_acc, col_acc = totals
        slot_number = block_step * block_tiles + lane_index
        is_live = slot_number < live_count
        clamped = jnp.minimum(slot_number, max_tiles - 1)
        values = jnp.take(packed, clamped, axis=0).astype(jnp.float32)
        row_part = jnp.sum(values, axis=2)
        col_part = jnp.sum(values, axis=1)
        row_part = jnp.where(is_live[:, None], row_part, 0.0)
        col_part = jnp.where(is_live[:, None], col_part, 0.0)
        row_acc = row_acc.at[jnp.take(own_rows, clamped)].add(row_part)
        col_acc = col_acc.at[jnp.take(own_cols, clamped)].add(col_part)
        return (row_acc, col_acc)

    degree_blocks = (live_count + block_tiles - 1) // block_tiles
    row_acc, col_acc = lax.fori_loop(
        jnp.int32(0),
        degree_blocks,
        degree_step,
        (
            jnp.zeros((row_tiles, tile_size), jnp.float32),
            jnp.zeros((col_tiles, tile_size), jnp.float32),
        ),
    )
    col_part_flat = col_acc.reshape(col_tiles * tile_size)
    col_share = lax.psum_scatter(col_part_flat, "row", scatter_dimension=0, tiled=True)
    scaled = (lax.rsqrt(1.0 + col_share)[:, None] * features.astype(jnp.float32)).astype(
        jnp.bfloat16
    )
    gathered = lax.all_gather(scaled, "row", axis=0, tiled=True)
    feature_tiles = gathered.reshape(col_tiles, tile_size, feat_width)
    list_length = packed.shape[0]

    def product_step(block_step, partial_value):
        logical = block_step * block_tiles + lane_index
        is_live = logical < live_count
        is_upper = logical >= live_count
        source = jnp.where(is_upper, logical - live_count, logical)
        source = jnp.clip(source, 0, list_length - 1)
        slot_number = jnp.minimum(is_upper.astype(jnp.int32), 1 - 1)
        tile_block = jnp.take(packed, source, axis=0)
        tile_block = jnp.where(is_live[:, None, None], tile_block, jnp.zeros((), jnp.bfloat16))
        inputs = jnp.take(feature_tiles, jnp.take(own_cols, source), axis=0)
        products = jnp.einsum(
            "bpq,bqf->bpf", tile_block, inputs, preferred_element_type=jnp.float32
        )
        return partial_value.at[slot_number, jnp.take(own_rows, source)].add(products)

    product_blocks = (live_count + block_tiles - 1) // block_tiles
    initial = jnp.zeros((1, row_tiles, tile_size, feat_width), jnp.float32)
    partial_value = lax.fori_loop(jnp.int32(0), product_blocks, product_step, initial)
    own_sum = partial_value[0]
    row_part_flat = row_acc.reshape(row_tiles * tile_size)
    summed, degree_share = (
        lax.psum_scatter(
            own_sum.reshape(row_tiles * tile_size, feat_width),
            "col",
            scatter_dimension=0,
            tiled=True,
        ),
        lax.psum_scatter(row_part_flat, "col", scatter_dimension=0, tiled=True),
    )
    aggregated = (lax.rsqrt(1.0 + degree_share)[:, None] * summed).astype(jnp.bfloat16)
    preact = jnp.dot(aggregated, weight, preferred_element_type=jnp.float32) + bias
    logistic = jax.nn.sigmoid(preact)
    hidden = (preact * logistic).astype(jnp.bfloat16)
    preact_grad = (
        cotangent.astype(jnp.float32) * logistic * (1.0 + preact * (1.0 - logistic))
    ).astype(jnp.bfloat16)
    weight_part = jnp.einsum(
        "nf,nh->fh", aggregated, preact_grad, preferred_element_type=jnp.float32
    )
    bias_part = jnp.sum(preact_grad.astype(jnp.float32), axis=0)
    weight_sum, bias_sum = lax.psum((weight_part, bias_part), ("row", "col"))
    inverse_root = lax.rsqrt(jnp.float32(summed.shape[0] * row_count * col_count))
    return (hidden, weight_sum * inverse_root, bias_sum * inverse_root)


def solution(mesh):
    placed = (
        P(("col", "row"), None),
        P(),
        P(),
        P(("row", "col"), None),
        P("row", "col", None, None, None),
        P("row", "col", None, None),
        P("row", "col"),
        P(),
    )
    return jax.shard_map(
        body,
        mesh=mesh,
        in_specs=placed,
        out_specs=(P(("row", "col"), None), P(), P()),
        check_vma=False,
    )
```

profile of v0, /device:TPU:2, one launch (start us, length us, event | category | flops | bytes accessed | tf_op | source)
XLA Modules:
  0.0 723.7 jit_solution(14614431443404107920)
XLA Ops:
  7.2 0.0 copy-start
  7.2 0.0 all-gather.2.cloned.1.call-start
  7.9 0.8 slice_add_fusion
  8.7 2.0 gather_fusion.8
  10.7 2.0 gather_fusion.7
  12.7 0.0 copy-start.8
  12.7 0.0 copy-start.4
  12.7 0.0 copy-start.5
  12.7 9.5 %while.24 = (s32[]{:T(128)}, f32[8,128]{1,0:T(8,128)S(1)}, f32[32,128]{1,0:T(8,128)S(1)}, s32[]{:T(128)}, s32[256]{0:T(256)S(1)}, /*index=5*/s32[]{:T(128)}, bf1...) while((s32[]{:T(128)}, f32[8,128]{1,0:T(8,128)S(1)}, ...), condition=%wide.region_5.9_spmd.clone, body=%wide.region_0.8_spmd.clone.sunk | while | flops 4213635 | bytes 6451793 | solution.py:44
  12.8 0.7 compare_and_fusion.6
  13.4 0.8 gather_fusion.1
  14.2 0.8 gather_fusion
  15.0 4.3 gather_fusion.2
  19.4 0.9 convert_reduce_fusion.4
  20.2 1.0 scatter_custom_fusion.15
  21.2 1.0 scatter_custom_fusion.16
  22.2 122.7 %all-reduce.1 = f32[4096]{0:T(1024)S(1)} all-reduce(f32[4096]{0:T(1024)S(1)} %bitcast.44), channel_id=3, replica_groups=mesh['row'=32,'col'=8] {'row'}, use_global_device_ids=true, to_apply=%region_7.11.clone | all-reduce | flops 4096 | bytes 32768
  145.0 0.6 dynamic-slice.2
  146.2 0.1 fusion.31
  146.3 0.7 multiply_convert_fusion.3
  147.0 0.0 all-gather.2.cloned.1.call-update
  147.0 0.0 reduce-scatter.2.cloned.1.call-start
  147.1 74.5 %all-gather.2.cloned.1.call-done = bf16[4096,128]{1,0:T(8,128)(2,1)} async-done(((bf16[128,128]{1,0:T(8,128)(2,1)}), bf16[4096,128]{1,0:T(8,128)(2,1)}) %all-gather.2.cloned.1.call-update) | async-done | bytes 1048592 | tf_op jit(solution)/shard_map/all_gather | solution.py:58
  221.6 0.0 copy-start.7
  221.6 0.0 copy-start.6
  221.6 24.0 %while.25 = (s32[]{:T(128)}, f32[1,8,128,128]{3,2,1,0:T(8,128)S(1)}, s32[]{:T(128)}, s32[]{:T(128)}, s32[256]{0:T(256)S(1)}, /*index=5*/bf16[256,128,128]{2,1,0:...) while((s32[]{:T(128)}, f32[1,8,128,128]{3,2,1,0:T(8,128)S(1)}, ...), condition=%wide.region_10.14_spmd.clone, body=%wide.region_8.13_spmd.clone.sunk | while | flops 272634240 | bytes 41956408 | solution.py:79
  221.6 0.7 compare_and_fusion.7
  222.4 0.8 gather_fusion.5
  223.2 0.8 gather_fusion.3
  224.0 0.7 fusion.44
  224.7 2.2 gather_fusion.6
  226.8 5.7 gather_fusion.4
  232.5 4.3 fusion.45
  236.8 8.8 %scatter_fusion = f32[8,128,128]{2,1,0:T(8,128)S(1)} fusion(f32[8,128,128]{2,1,0:T(8,128)S(1)} %bitcast.39, s32[64]{0:T(128)S(1)} %fusion.44, f32[64,128,128]{2,1,0:T(8,128)} %fusion.45), kind=kCustom, calls=%fused_computation.11.clone.clone.1 | custom fusion | flops 1048576 | bytes 12583168 | tf_op jit(solution)/shard_map/while/body/scatter-add | solution.py:75
  245.6 0.8 copy-done.1
  246.4 0.0 reduce-scatter.2.cloned.1.call-update
  246.4 0.0 all-reduce.4.cloned.1.call-start
  246.5 0.6 dynamic-slice
  247.7 43.6 %all-reduce = f32[1024]{0:T(1024)S(1)} all-reduce(f32[1024]{0:T(1024)S(1)} %bitcast.45), channel_id=2, replica_groups=mesh['row'=32,'col'=8] {'col'}, use_global_device_ids=true, to_apply=%region_6.10.clone | all-reduce | flops 1024 | bytes 8192
  291.3 0.1 fusion.32
  291.4 102.7 %reduce-scatter.2.cloned.1.call-done = f32[128,128]{1,0:T(8,128)} async-done(((f32[1024,128]{1,0:T(8,128)}), f32[128,128]{1,0:T(8,128)}) %reduce-scatter.2.cloned.1.call-update) | async-done | bytes 65552 | tf_op jit(solution)/shard_map/reduce_scatter | solution.py:83
  394.1 1.7 convert_reduce_fusion.2
  395.8 73.9 %psum.15 = f32[256]{0:T(256)S(1)} all-reduce(f32[256]{0:T(256)S(1)} %get-tuple-element.182), channel_id=1, replica_groups=mesh['row'=32,'col'=8] {'row','col'}, use_global_device_ids=true, to_apply=%region_14.18 | all-reduce | flops 256 | bytes 2048 | tf_op jit(solution)/shard_map/psum | solution.py:102
  469.8 1.8 fusion.33
  471.6 0.0 all-reduce.4.cloned.1.call-update
  471.6 0.6 broadcast_multiply_fusion.1
  472.1 243.5 %all-reduce.4.cloned.1.call-done = f32[128,256]{1,0:T(8,128)} async-done(((f32[128,256]{1,0:T(8,128)}), f32[128,256]{1,0:T(8,128)}) %all-reduce.4.cloned.1.call-update) | async-done | bytes 131088 | tf_op jit(solution)/shard_map/psum | solution.py:102
  715.6 1.6 broadcast_multiply_fusion
  (25 shorter events, 0.1 us)
Async XLA Ops:
  7.2 386.9 %copy-start = (bf16[128,256]{1,0:T(8,128)(2,1)S(1)}, bf16[128,256]{1,0:T(8,128)(2,1)}, u32[]{:S(2)}) copy-start(bf16[128,256]{1,0:T(8,128)(2,1)} %param.19) | copy-start | bytes 196612
  7.2 214.3 %all-gather.2.cloned.1.call-start = ((), (), s32[]{:S(2)}) async-start(), calls=%async_computation.1 | async-start | bytes 1081344 | tf_op jit(solution)/shard_map/all_gather | solution.py:58
  12.7 132.3 %copy-start.8 = (u32[256]{0:T(256)S(1)}, u32[256]{0:T(256)}, u32[]{:S(2)}) copy-start(u32[256]{0:T(256)} %constant.133) | copy-start | bytes 3076
  12.7 133.6 %copy-start.4 = (bf16[128,128]{1,0:T(8,128)(2,1)S(1)}, bf16[128,128]{1,0:T(8,128)(2,1)}, u32[]{:S(2)}) copy-start(bf16[128,128]{1,0:T(8,128)(2,1)} %param.18) | copy-start | bytes 98308
  12.7 381.4 %copy-start.5 = (bf16[128,256]{1,0:T(8,128)(2,1)S(1)}, bf16[128,256]{1,0:T(8,128)(2,1)}, u32[]{:S(2)}) copy-start(bf16[128,256]{1,0:T(8,128)(2,1)} %param.21) | copy-start | bytes 196612
  147.0 247.1 %reduce-scatter.2.cloned.1.call-start = ((), (), s32[]{:S(2)}) async-start(), calls=%async_computation.2 | async-start | bytes 589824 | tf_op jit(solution)/shard_map/reduce_scatter | solution.py:83
  221.6 24.9 %copy-start.7 = (u32[256]{0:T(256)S(1)}, u32[256]{0:T(256)}, u32[]{:S(2)}) copy-start(u32[256]{0:T(256)} %constant.129) | copy-start | bytes 3076
  221.6 172.5 %copy-start.6 = (f32[256]{0:T(256)S(1)}, f32[256]{0:T(256)}, u32[]{:S(2)}) copy-start(f32[256]{0:T(256)} %param.20) | copy-start | bytes 3076
  221.6 3.1 copy-start.2
  226.8 5.7 copy-start.3
  245.6 0.8 copy-start.1
  246.4 469.2 %all-reduce.4.cloned.1.call-start = ((), (), s32[]{:S(2)}) async-start(), calls=%async_computation.3 | async-start | bytes 262144 | tf_op jit(solution)/shard_map/psum | solution.py:102
Sparse Core Ops, SparseCore 0:
  147.1 74.3 all-gather.1
  246.6 147.4 reduce-scatter.1
  471.7 243.8 all-reduce.3
where the time goes:
time: 725 us; the launch traced here: 724 us
  waiting for transfers between devices  421 us (58%)
  blocking collectives  240 us (33%)
  local copies, waits for them, and re-layouts  21.3 us (3%)
  other arithmetic  17.5 us (2%)
  between operations  15.9 us (2%)
  matrix products  7.81 us (1%)
    psum x1, waiting for transfers between devices, body(): weight_sum, bias_sum = lax.psum((weight_part, bias_part), ('row', 'col'))  243 us
    unnamed x2, blocking collectives  166 us
    reduce_scatter x1, waiting for transfers between devices, body(): lax.psum_scatter(own_sum.reshape(row_tiles * tile_size, feat_width), 'col...  103 us
    all_gather x1, waiting for transfers between devices, body(): gathered = lax.all_gather(scaled, 'row', axis=0, tiled=True)  74.5 us
    psum x1, blocking collectives, body(): weight_sum, bias_sum = lax.psum((weight_part, bias_part), ('row', 'col'))  73.9 us
  transfers between devices with their start and end apart: 3, of which 3 were waited for; matrix products, arithmetic and copies ran while one was open for 0% of the time, Pallas kernels for 0%

commit v1 on v0

--- a/solution.py
+++ b/solution.py
@@ -9,6 +9,12 @@
 
 
 def body(features, weight, bias, cotangent, tile_values, tile_pos, tile_count, block_perm):
+
+    def grid_obtain(x_local):
+        for k0 in ("row", "col"):
+            x_local = lax.psum(x_local, k0)
+        return x_local
+
     row_count = lax.axis_size("row")
     col_count = lax.axis_size("col")
     row_index = lax.axis_index("row")
@@ -99,7 +105,7 @@
         "nf,nh->fh", aggregated, preact_grad, preferred_element_type=jnp.float32
     )
     bias_part = jnp.sum(preact_grad.astype(jnp.float32), axis=0)
-    weight_sum, bias_sum = lax.psum((weight_part, bias_part), ("row", "col"))
+    weight_sum, bias_sum = grid_obtain((weight_part, bias_part))
     inverse_root = lax.rsqrt(jnp.float32(summed.shape[0] * row_count * col_count))
     return (hidden, weight_sum * inverse_root, bias_sum * inverse_root)
 

time: 725 us -> 703 us (0.970)
  waiting for transfers between devices: 421 us -> 396 us
    psum x1 -> x2, waiting for transfers between devices: 243 us -> 218 us  [grid_obtain(): x_local = lax.psum(x_local, k0)]
    psum x1 -> x2, blocking collectives: 73.9 us -> 74 us  [grid_obtain(): x_local = lax.psum(x_local, k0)]
  transfers between devices with their start and end apart: 3 -> 4, of which waited for: 3 -> 4; matrix products, arithmetic and copies ran while one was open for 0% -> 0% of each run, Pallas kernels for 0% -> 0%
where the time goes in v1:
time: 703 us; the launch traced here: 699 us
  waiting for transfers between devices  396 us (56%)
  blocking collectives  240 us (34%)
  local copies, waits for them, and re-layouts  21.3 us (3%)
  other arithmetic  17.5 us (2%)
  between operations  15.9 us (2%)
  matrix products  7.81 us (1%)
    psum x2, waiting for transfers between devices, grid_obtain(): x_local = lax.psum(x_local, k0)  218 us
    unnamed x2, blocking collectives  166 us
    reduce_scatter x1, waiting for transfers between devices, body(): lax.psum_scatter(own_sum.reshape(row_tiles * tile_size, feat_width), 'col...  103 us
    all_gather x1, waiting for transfers between devices, body(): gathered = lax.all_gather(scaled, 'row', axis=0, tiled=True)  74.5 us
    psum x2, blocking collectives, grid_obtain(): x_local = lax.psum(x_local, k0)  74 us
  transfers between devices with their start and end apart: 4, of which 4 were waited for; matrix products, arithmetic and copies ran while one was open for 0% of the time, Pallas kernels for 0%

profile of v1, /device:TPU:2, one launch (start us, length us, event | category | flops | bytes accessed | tf_op | source)
XLA Modules:
  0.0 698.9 jit_solution(10427341483074446523)
XLA Ops:
  7.2 0.0 copy-start
  7.2 0.0 all-gather.2.cloned.1.call-start
  7.9 0.8 slice_add_fusion
  8.7 2.0 gather_fusion.8
  10.7 2.0 gather_fusion.7
  12.7 0.0 copy-start.8
  12.7 9.5 %while.24 = (s32[]{:T(128)}, f32[8,128]{1,0:T(8,128)S(1)}, f32[32,128]{1,0:T(8,128)S(1)}, s32[]{:T(128)}, s32[256]{0:T(256)S(1)}, /*index=5*/s32[]{:T(128)}, bf1...) while((s32[]{:T(128)}, f32[8,128]{1,0:T(8,128)S(1)}, ...), condition=%wide.region_5.9_spmd.clone, body=%wide.region_0.8_spmd.clone.sunk | while | flops 4213635 | bytes 6451793 | solution.py:50
  12.8 0.7 compare_and_fusion.6
  13.4 0.8 gather_fusion.1
  14.2 0.8 gather_fusion
  15.0 4.3 gather_fusion.2
  19.4 0.9 convert_reduce_fusion.4
  20.2 1.0 scatter_custom_fusion.15
  21.2 1.0 scatter_custom_fusion.16
  22.2 122.7 %all-reduce.1 = f32[4096]{0:T(1024)S(1)} all-reduce(f32[4096]{0:T(1024)S(1)} %bitcast.44), channel_id=3, replica_groups=mesh['row'=32,'col'=8] {'row'}, use_global_device_ids=true, to_apply=%region_7.11.clone | all-reduce | flops 4096 | bytes 32768
  145.0 0.6 dynamic-slice.2
  146.2 0.1 fusion.31
  146.3 0.7 multiply_convert_fusion.3
  147.0 0.0 all-gather.2.cloned.1.call-update
  147.0 0.0 reduce-scatter.2.cloned.1.call-start
  147.1 74.5 %all-gather.2.cloned.1.call-done = bf16[4096,128]{1,0:T(8,128)(2,1)} async-done(((bf16[128,128]{1,0:T(8,128)(2,1)}), bf16[4096,128]{1,0:T(8,128)(2,1)}) %all-gather.2.cloned.1.call-update) | async-done | bytes 1048592 | tf_op jit(solution)/shard_map/all_gather | solution.py:64
  221.6 24.0 %while.25 = (s32[]{:T(128)}, f32[1,8,128,128]{3,2,1,0:T(8,128)S(1)}, s32[]{:T(128)}, s32[]{:T(128)}, s32[256]{0:T(256)S(1)}, /*index=5*/bf16[256,128,128]{2,1,0:...) while((s32[]{:T(128)}, f32[1,8,128,128]{3,2,1,0:T(8,128)S(1)}, ...), condition=%wide.region_10.14_spmd.clone, body=%wide.region_8.13_spmd.clone.sunk | while | flops 272634240 | bytes 41956408 | solution.py:85
  221.6 0.7 compare_and_fusion.7
  222.4 0.8 gather_fusion.5
  223.2 0.8 gather_fusion.3
  224.0 0.7 fusion.44
  224.7 2.2 gather_fusion.6
  226.8 5.7 gather_fusion.4
  232.5 4.3 fusion.45
  236.8 8.8 %scatter_fusion = f32[8,128,128]{2,1,0:T(8,128)S(1)} fusion(f32[8,128,128]{2,1,0:T(8,128)S(1)} %bitcast.39, s32[64]{0:T(128)S(1)} %fusion.44, f32[64,128,128]{2,1,0:T(8,128)} %fusion.45), kind=kCustom, calls=%fused_computation.11.clone.clone.1 | custom fusion | flops 1048576 | bytes 12583168 | tf_op jit(solution)/shard_map/while/body/scatter-add | solution.py:81
  245.6 0.8 copy-done.1
  246.4 0.0 reduce-scatter.2.cloned.1.call-update
  246.4 0.0 all-reduce.5.cloned.1.call-start
  246.5 0.6 dynamic-slice
  247.7 43.6 %all-reduce = f32[1024]{0:T(1024)S(1)} all-reduce(f32[1024]{0:T(1024)S(1)} %bitcast.45), channel_id=2, replica_groups=mesh['row'=32,'col'=8] {'col'}, use_global_device_ids=true, to_apply=%region_6.10.clone | all-reduce | flops 1024 | bytes 8192
  291.3 0.1 fusion.32
  291.4 102.7 %reduce-scatter.2.cloned.1.call-done = f32[128,128]{1,0:T(8,128)} async-done(((f32[1024,128]{1,0:T(8,128)}), f32[128,128]{1,0:T(8,128)}) %reduce-scatter.2.cloned.1.call-update) | async-done | bytes 65552 | tf_op jit(solution)/shard_map/reduce_scatter | solution.py:89
  394.1 1.7 convert_reduce_fusion.2
  395.8 1.8 fusion.33
  397.6 0.0 all-reduce.5.cloned.1.call-update
  397.6 0.0 all-reduce.7.cloned.1.call-start
  397.7 53.7 %psum.30 = f32[256]{0:T(256)S(1)} all-reduce(f32[256]{0:T(256)S(1)} %get-tuple-element.182), channel_id=1, replica_groups=mesh['row'=32,'col'=8] {'row'}, use_global_device_ids=true, to_apply=%region_15.19 | all-reduce | flops 256 | bytes 2048 | tf_op jit(solution)/shard_map/psum | solution.py:15
  451.4 20.3 %psum.31 = f32[256]{0:T(256)S(1)} all-reduce(f32[256]{0:T(256)S(1)} %psum.30), channel_id=1, replica_groups=mesh['row'=32,'col'=8] {'col'}, use_global_device_ids=true, to_apply=%region_16.20 | all-reduce | flops 256 | bytes 2048 | tf_op jit(solution)/shard_map/psum | solution.py:15
  471.7 131.2 %all-reduce.5.cloned.1.call-done = f32[128,256]{1,0:T(8,128)} async-done(((f32[128,256]{1,0:T(8,128)}), f32[128,256]{1,0:T(8,128)}) %all-reduce.5.cloned.1.call-update) | async-done | bytes 131088 | tf_op jit(solution)/shard_map/psum | solution.py:15
  602.8 0.0 all-reduce.7.cloned.1.call-update
  602.9 0.6 broadcast_multiply_fusion.1
  603.4 87.3 %all-reduce.7.cloned.1.call-done = f32[128,256]{1,0:T(8,128)} async-done(((f32[128,256]{1,0:T(8,128)}), f32[128,256]{1,0:T(8,128)}) %all-reduce.7.cloned.1.call-update) | async-done | bytes 131088 | tf_op jit(solution)/shard_map/psum | solution.py:15
  690.7 1.6 broadcast_multiply_fusion
  (29 shorter events, 0.2 us)
Async XLA Ops:
  7.2 386.9 %copy-start = (bf16[128,256]{1,0:T(8,128)(2,1)S(1)}, bf16[128,256]{1,0:T(8,128)(2,1)}, u32[]{:S(2)}) copy-start(bf16[128,256]{1,0:T(8,128)(2,1)} %param.19) | copy-start | bytes 196612
  7.2 214.3 %all-gather.2.cloned.1.call-start = ((), (), s32[]{:S(2)}) async-start(), calls=%async_computation.1 | async-start | bytes 1081344 | tf_op jit(solution)/shard_map/all_gather | solution.py:64
  12.7 132.3 %copy-start.8 = (u32[256]{0:T(256)S(1)}, u32[256]{0:T(256)}, u32[]{:S(2)}) copy-start(u32[256]{0:T(256)} %constant.133) | copy-start | bytes 3076
  12.7 133.6 %copy-start.4 = (bf16[128,128]{1,0:T(8,128)(2,1)S(1)}, bf16[128,128]{1,0:T(8,128)(2,1)}, u32[]{:S(2)}) copy-start(bf16[128,128]{1,0:T(8,128)(2,1)} %param.18) | copy-start | bytes 98308
  12.7 381.4 %copy-start.5 = (bf16[128,256]{1,0:T(8,128)(2,1)S(1)}, bf16[128,256]{1,0:T(8,128)(2,1)}, u32[]{:S(2)}) copy-start(bf16[128,256]{1,0:T(8,128)(2,1)} %param.21) | copy-start | bytes 196612
  147.0 247.1 %reduce-scatter.2.cloned.1.call-start = ((), (), s32[]{:S(2)}) async-start(), calls=%async_computation.2 | async-start | bytes 589824 | tf_op jit(solution)/shard_map/reduce_scatter | solution.py:89
  221.6 24.9 %copy-start.7 = (u32[256]{0:T(256)S(1)}, u32[256]{0:T(256)}, u32[]{:S(2)}) copy-start(u32[256]{0:T(256)} %constant.129) | copy-start | bytes 3076
  221.6 172.5 %copy-start.6 = (f32[256]{0:T(256)S(1)}, f32[256]{0:T(256)}, u32[]{:S(2)}) copy-start(f32[256]{0:T(256)} %param.20) | copy-start | bytes 3076
  221.6 3.1 copy-start.2
  226.8 5.7 copy-start.3
  245.6 0.8 copy-start.1
  246.4 356.4 %all-reduce.5.cloned.1.call-start = ((), (), s32[]{:S(2)}) async-start(), calls=%async_computation.3 | async-start | bytes 262144 | tf_op jit(solution)/shard_map/psum | solution.py:15
  397.6 293.1 %all-reduce.7.cloned.1.call-start = ((), (), s32[]{:S(2)}) async-start(), calls=%async_computation.4 | async-start | bytes 262144 | tf_op jit(solution)/shard_map/psum | solution.py:15
Sparse Core Ops, SparseCore 0:
  147.1 74.3 all-gather.1
  246.6 147.4 reduce-scatter.1
  397.7 205.0 all-reduce.4
  605.3 85.4 all-reduce.6
